TPU v7x, 32 devices: a whole 2x2x4 slice. The times are simulated.
32 devices in a mesh: grp: 8 (over y, x, core), leaf: 4 (over z).
Axes of the slice: x: 2, y: 2, z: 4, core: 2. Of those that a mesh axis runs over, the one named last changes fastest.
Arguments:
- labels: int32 [16384], P(('grp', 'leaf')), may hold values from 0 to 255
- leaf_inverse: float32 [16384, 512], P(('grp', 'leaf')), may hold values from -1 to 4
- leaf_basis: float32 [16384, 128], P(('grp', 'leaf')), may hold values from -0.25 to 0.25
- leaf_solved: float32 [16384, 128], P(('grp', 'leaf')), may hold values from -0.5 to 0.5
- group_capacitance: float32 [4096, 512], P(('grp', 'leaf')), may hold values from -1 to 4
- top_basis: float32 [16384, 128], P(('grp', 'leaf')), may hold values from -0.125 to 0.125
- top_solved: float32 [16384, 128], P(('grp', 'leaf')), may hold values from -0.5 to 0.5
- top_capacitance: float32 [1024, 1024], P('grp'), may hold values from -1 to 4
Outputs:
- dual_box: float32 [16384, 256], P(('grp', 'leaf'))
- scaled_dual: float32 [16384, 256], P(('grp', 'leaf'))
All inputs are finite; a program needn't handle non-finite values.
Results may differ from a plain program's by a relative error of at most 0.0003.
Values sent between devices are 32-bit elements; how exact they have to be, the bound alone decides.
A program may use at most 64 MiB of HBM per device.

v0:
```python
import jax
import jax.numpy as jnp
from jax import lax
from jax.sharding import PartitionSpec as P

CLASSES = 256
ITERS = 2
high = lax.Precision.HIGHEST


def matmul(left, right):
    return jnp.dot(left, right, precision=high, preferred_element_type=jnp.float32)


def project_rows(basis, values):
    return lax.dot_general(
        basis, values, (((0,), (0,)), ((), ())), precision=high, preferred_element_type=jnp.float32
    )


def column_product(matrix, piece):
    return matmul(matrix, piece)


def shards(
    labels,
    leaf_inverse,
    leaf_basis,
    leaf_solved,
    group_capacitance,
    top_basis,
    top_solved,
    top_capacitance,
):
    columns = lax.broadcasted_iota(jnp.int32, (labels.shape[0], CLASSES), 1)
    label_sign = jnp.where(labels[:, None] == columns, 1.0, -1.0).astype(jnp.float32)
    dual_box = jnp.zeros((labels.shape[0], CLASSES), jnp.float32)
    scaled_dual = jnp.zeros((labels.shape[0], CLASSES), jnp.float32)
    for iteration in range(ITERS):
        rhs = label_sign * (1.0 + 1.0 * (dual_box - scaled_dual))
        local = matmul(leaf_inverse, rhs)
        coeffs = project_rows(leaf_basis, local)
        group_coef = column_product(
            group_capacitance, lax.all_gather(coeffs, "leaf", axis=0, tiled=True)
        )
        inner = local - matmul(leaf_solved, group_coef)
        partial_proj = project_rows(top_basis, inner)
        share = lax.psum_scatter(partial_proj, "leaf", scatter_dimension=1, tiled=True)
        share_coef = column_product(
            top_capacitance, lax.all_gather(share, "grp", axis=0, tiled=True)
        )
        top_coef = lax.all_gather(share_coef, "leaf", axis=1, tiled=True)
        solved = inner - matmul(top_solved, top_coef)
        moved = scaled_dual + label_sign * solved
        dual_box = jnp.clip(moved, 0.0, 1.0)
        scaled_dual = moved - dual_box
    return (dual_box, scaled_dual)


def solution(mesh):
    return jax.shard_map(
        shards,
        mesh=mesh,
        in_specs=(
            P(("grp", "leaf")),
            P(("grp", "leaf"), None),
            P(("grp", "leaf"), None),
            P(("grp", "leaf"), None),
            P(("grp", "leaf"), None),
            P(("grp", "leaf"), None),
            P(("grp", "leaf"), None),
            P("grp", None),
        ),
        out_specs=(P(("grp", "leaf"), None), P(("grp", "leaf"), None)),
        check_vma=False,
    )
```

profile of v0, /device:TPU:0, one launch (start us, length us, event | category | flops | bytes accessed | tf_op | source)
XLA Modules:
  0.0 148.3 jit_solution(11948927339360543717)
XLA Ops:
  7.2 0.0 copy-start
  7.2 0.0 copy-start.2
  7.2 0.0 reduce-scatter.3.cloned.1.call-start
  7.2 1.2 copy-done
  8.4 1.8 %fusion.5 = f32[256,512]{1,0:T(8,128)S(1)} fusion(f32[512,512]{1,0:T(8,128)S(1)} %copy-done, s32[512]{0:T(512)} %param.8), kind=kOutput, calls=%fused_computation.16 | convolution fusion | flops 805568512 | bytes 1574912 | tf_op jit(solution)/shard_map/dot_general | solution.py:12
  10.2 0.0 copy-done.2
  10.2 0.6 convolution_bitcast_fusion.3
  10.8 0.0 copy-start.3
  10.8 17.5 %all_gather.18 = f32[512,256]{0,1:T(8,128)S(1)} all-gather(f32[128,256]{0,1:T(8,128)S(1)} %convolution_bitcast_fusion.3), channel_id=1, replica_groups=mesh['grp'=8,'leaf'=4] {'leaf'}, dimensions={0}, use_global_device_ids=true | all-gather | bytes 655360 | tf_op jit(solution)/shard_map/all_gather | solution.py:44
  28.3 0.0 copy-done.3
  28.3 0.0 copy-start.5
  28.3 0.6 fusion.22
  28.9 0.4 copy-done.5
  29.2 0.0 copy-start.4
  29.2 0.6 convolution_subtract_fusion.3
  29.8 0.4 copy-done.4
  30.2 0.0 copy-start.1
  30.2 1.2 convolution_bitcast_fusion.2
  31.4 0.0 reduce-scatter.3.cloned.1.call-update
  31.5 0.0 reduce-scatter.5.cloned.1.call-start
  31.5 21.3 %reduce-scatter.3.cloned.1.call-done = f32[128,64]{0,1:T(8,128)} async-done(((f32[128,256]{0,1:T(8,128)}), f32[128,64]{0,1:T(8,128)}) %reduce-scatter.3.cloned.1.call-update) | async-done | bytes 32784 | tf_op jit(solution)/shard_map/reduce_scatter | solution.py:48
  52.8 10.0 %all_gather.19 = f32[1024,64]{0,1:T(8,128)S(1)} all-gather(f32[128,64]{0,1:T(8,128)} %reduce-scatter.3.cloned.1.call-done), channel_id=1, replica_groups=mesh['grp'=8,'leaf'=4] {'grp'}, dimensions={0}, use_global_device_ids=true | all-gather | bytes 294912 | tf_op jit(solution)/shard_map/all_gather | solution.py:50
  62.8 0.0 copy-done.1
  62.8 0.0 copy-start.7
  62.8 0.7 convolution_bitcast_fusion.5
  63.5 0.0 copy-start.9
  63.5 13.5 %all_gather.20 = f32[128,256]{0,1:T(8,128)S(1)} all-gather(f32[128,64]{0,1:T(8,128)S(1)} %convolution_bitcast_fusion.5), channel_id=1, replica_groups=mesh['grp'=8,'leaf'=4] {'leaf'}, dimensions={1}, use_global_device_ids=true | all-gather | bytes 163840 | tf_op jit(solution)/shard_map/all_gather | solution.py:52
  77.0 0.0 copy-done.7
  77.0 0.0 copy-done.9
  77.0 0.6 fusion.4
  77.6 1.2 fusion.8
  78.8 0.6 convolution_bitcast_fusion.1
  79.4 14.8 %all_gather.21 = f32[512,256]{0,1:T(8,128)S(1)} all-gather(f32[128,256]{0,1:T(8,128)S(1)} %convolution_bitcast_fusion.1), channel_id=1, replica_groups=mesh['grp'=8,'leaf'=4] {'leaf'}, dimensions={0}, use_global_device_ids=true | all-gather | bytes 655360 | tf_op jit(solution)/shard_map/all_gather | solution.py:44
  94.1 0.0 copy-start.6
  94.1 0.6 fusion.23
  94.7 0.4 copy-done.6
  95.1 0.6 convolution_subtract_fusion.1
  95.7 1.2 convolution_bitcast_fusion
  96.9 0.0 reduce-scatter.5.cloned.1.call-update
  96.9 17.6 %reduce-scatter.5.cloned.1.call-done = f32[128,64]{0,1:T(8,128)} async-done(((f32[128,256]{0,1:T(8,128)}), f32[128,64]{0,1:T(8,128)}) %reduce-scatter.5.cloned.1.call-update) | async-done | bytes 32784 | tf_op jit(solution)/shard_map/reduce_scatter | solution.py:48
  114.5 10.0 %all_gather.22 = f32[1024,64]{0,1:T(8,128)S(1)} all-gather(f32[128,64]{0,1:T(8,128)} %reduce-scatter.5.cloned.1.call-done), channel_id=1, replica_groups=mesh['grp'=8,'leaf'=4] {'grp'}, dimensions={0}, use_global_device_ids=true | all-gather | bytes 294912 | tf_op jit(solution)/shard_map/all_gather | solution.py:50
  124.5 0.0 copy-start.8
  124.5 0.7 convolution_bitcast_fusion.4
  125.2 13.6 %all_gather.23 = f32[128,256]{0,1:T(8,128)S(1)} all-gather(f32[128,64]{0,1:T(8,128)S(1)} %convolution_bitcast_fusion.4), channel_id=1, replica_groups=mesh['grp'=8,'leaf'=4] {'leaf'}, dimensions={1}, use_global_device_ids=true | all-gather | bytes 163840 | tf_op jit(solution)/shard_map/all_gather | solution.py:52
  138.8 0.0 copy-done.8
  138.8 0.7 fusion.16
  139.5 1.0 copy.11
  140.5 1.0 copy.10
Async XLA Ops:
  7.2 1.2 copy-start
  7.2 3.0 %copy-start.2 = (f32[512,128]{1,0:T(8,128)S(1)}, f32[512,128]{1,0:T(8,128)}, u32[]{:S(2)}) copy-start(f32[512,128]{1,0:T(8,128)} %param.10) | copy-start | bytes 786436
  7.2 45.6 %reduce-scatter.3.cloned.1.call-start = ((), (), s32[]{:S(2)}) async-start(), calls=%async_computation.2 | async-start | bytes 163840 | tf_op jit(solution)/shard_map/reduce_scatter | solution.py:48
  10.8 17.5 %copy-start.3 = (f32[128,512]{1,0:T(8,128)S(1)}, f32[128,512]{1,0:T(8,128)}, u32[]{:S(2)}) copy-start(f32[128,512]{1,0:T(8,128)} %param.12) | copy-start | bytes 786436
  28.3 1.0 copy-start.5
  29.2 0.9 copy-start.4
  30.2 32.6 %copy-start.1 = (f32[128,1024]{1,0:T(8,128)S(1)}, f32[128,1024]{1,0:T(8,128)}, u32[]{:S(2)}) copy-start(f32[128,1024]{1,0:T(8,128)} %param.15) | copy-start | bytes 1572868
  31.5 83.1 %reduce-scatter.5.cloned.1.call-start = ((), (), s32[]{:S(2)}) async-start(), calls=%async_computation.3 | async-start | bytes 163840 | tf_op jit(solution)/shard_map/reduce_scatter | solution.py:48
  62.8 14.1 %copy-start.7 = (f32[512,128]{1,0:T(8,128)S(1)}, f32[512,128]{1,0:T(8,128)}, u32[]{:S(2)}) copy-start(f32[512,128]{1,0:T(8,128)} %param.14) | copy-start | bytes 786436
  63.5 13.5 %copy-start.9 = (s32[512]{0:T(512)S(1)}, s32[512]{0:T(512)}, u32[]{:S(2)}) copy-start(s32[512]{0:T(512)} %param.8) | copy-start | bytes 6148
  94.1 1.0 copy-start.6
  124.5 14.3 %copy-start.8 = (f32[512,128]{1,0:T(8,128)S(1)}, f32[512,128]{1,0:T(8,128)}, u32[]{:S(2)}) copy-start(f32[512,128]{1,0:T(8,128)} %param.14) | copy-start | bytes 786436
Sparse Core Ops, SparseCore 0:
  31.6 21.1 reduce-scatter.2
  97.1 17.4 reduce-scatter.4
where the time goes:
time: 149 us; the launch traced here: 148 us
  blocking collectives  79.3 us (53%)
  waiting for transfers between devices  38.9 us (26%)
  between operations  14.2 us (10%)
  matrix products  11.5 us (8%)
  local copies, waits for them, and re-layouts  4.27 us (3%)
    reduce_scatter x2, waiting for transfers between devices, shards(): lax.psum_scatter(partial_proj, 'leaf', scatter_dimension=1, tiled=True)  38.9 us
    all_gather x2, blocking collectives, shards(): lax.all_gather(coeffs, 'leaf', axis=0, tiled=True)  32.3 us
    all_gather x2, blocking collectives, shards(): top_coef = lax.all_gather(share_coef, 'leaf', axis=1, tiled=True)  27.1 us
    all_gather x2, blocking collectives, shards(): lax.all_gather(share, 'grp', axis=0, tiled=True)  20 us
    dot_general x10, matrix products, matmul(): jnp.dot(left, right, precision=high, preferred_element_type=jnp.float32)  7.88 us
    unnamed x22, local copies, waits for them, and re-layouts  4.27 us
    dot_general x4, matrix products, project_rows(): lax.dot_general(basis, values, (((0,), (0,)), ((), ())), precision=high,...  3.65 us
  transfers between devices with their start and end apart: 2, of which 2 were waited for; matrix products, arithmetic and copies ran while one was open for 0% of the time, Pallas kernels for 0%

commit v1 on v0

--- a/solution.py
+++ b/solution.py
@@ -6,6 +6,19 @@
 CLASSES = 256
 ITERS = 2
 high = lax.Precision.HIGHEST
+
+
+def ring_gather(x, axis, dim):
+    ways = lax.axis_size(axis)
+    up = [(d, (d + 1) % ways) for d in range(ways)]
+    down = [(d, (d - 1) % ways) for d in range(ways)]
+    earlier, later = ([x], [x])
+    for _ in range(ways // 2):
+        earlier.append(lax.ppermute(earlier[-1], axis, up))
+    for _ in range((ways - 1) // 2):
+        later.append(lax.ppermute(later[-1], axis, down))
+    line = jnp.concatenate([*earlier[::-1], *later[1:]], axis=dim)
+    return jnp.roll(line, (lax.axis_index(axis) - ways // 2) * x.shape[dim], axis=dim)
 
 
 def matmul(left, right):
@@ -46,9 +59,7 @@
         inner = local - matmul(leaf_solved, group_coef)
         partial_proj = project_rows(top_basis, inner)
         share = lax.psum_scatter(partial_proj, "leaf", scatter_dimension=1, tiled=True)
-        share_coef = column_product(
-            top_capacitance, lax.all_gather(share, "grp", axis=0, tiled=True)
-        )
+        share_coef = column_product(top_capacitance, ring_gather(share, "grp", 0))
         top_coef = lax.all_gather(share_coef, "leaf", axis=1, tiled=True)
         solved = inner - matmul(top_solved, top_coef)
         moved = scaled_dual + label_sign * solved

time: 149 us -> 165 us (1.11)
  blocking collectives: 79.3 us -> 60 us
  waiting for transfers between devices: 38.9 us -> 57 us
  starting transfers between devices: 0.08 us -> 15.7 us
    all_gather x2 -> x0, blocking collectives: 20 us -> none  [shards(): lax.all_gather(share, 'grp', axis=0, tiled=True)]
    ppermute x0 -> x14, waiting for transfers between devices: none -> 18.7 us  [the longest x8 17.6 us: ring_gather(): earlier.append(lax.ppermute(earlier[-1], axis, up))]
    ppermute x0 -> x14, starting transfers between devices: none -> 15.7 us  [the longest x6 15.6 us: ring_gather(): later.append(lax.ppermute(later[-1], axis, down))]
    unnamed x22 -> x38, local copies, waits for them, and re-layouts: 4.27 us -> 5.84 us
  transfers between devices with their start and end apart: 2 -> 16, of which waited for: 2 -> 14; matrix products, arithmetic and copies ran while one was open for 0% -> 0% of each run, Pallas kernels for 0% -> 0%
where the time goes in v1:
time: 165 us; the launch traced here: 164 us
  blocking collectives  60 us (36%)
  waiting for transfers between devices  57 us (35%)
  starting transfers between devices  15.7 us (10%)
  between operations  14.3 us (9%)
  matrix products  11.5 us (7%)
  local copies, waits for them, and re-layouts  5.85 us (4%)
    reduce_scatter x2, waiting for transfers between devices, shards(): lax.psum_scatter(partial_proj, 'leaf', scatter_dimension=1, tiled=True)  38.3 us
    all_gather x2, blocking collectives, shards(): lax.all_gather(coeffs, 'leaf', axis=0, tiled=True)  33.3 us
    all_gather x2, blocking collectives, shards(): top_coef = lax.all_gather(share_coef, 'leaf', axis=1, tiled=True)  26.7 us
    ppermute x8, waiting for transfers between devices, ring_gather(): earlier.append(lax.ppermute(earlier[-1], axis, up))  17.6 us
    ppermute x6, starting transfers between devices, ring_gather(): later.append(lax.ppermute(later[-1], axis, down))  15.6 us
    dot_general x10, matrix products, matmul(): jnp.dot(left, right, precision=high, preferred_element_type=jnp.float32)  7.89 us
    unnamed x38, local copies, waits for them, and re-layouts  5.84 us
    dot_general x4, matrix products, project_rows(): lax.dot_general(basis, values, (((0,), (0,)), ((), ())), precision=high,...  3.65 us
  transfers between devices with their start and end apart: 16, of which 14 were waited for; matrix products, arithmetic and copies ran while one was open for 0% of the time, Pallas kernels for 0%

profile of v1, /device:TPU:0, one launch (start us, length us, event | category | flops | bytes accessed | tf_op | source)
XLA Modules:
  0.0 164.4 jit_solution(11296152370863721162)
XLA Ops:
  7.2 0.0 copy-start
  7.2 0.0 reduce-scatter.3.cloned.1.call-start
  7.2 1.2 copy-done
  8.4 1.8 %fusion.5 = f32[256,512]{1,0:T(8,128)S(1)} fusion(f32[512,512]{1,0:T(8,128)S(1)} %copy-done, s32[512]{0:T(512)} %param.10), kind=kOutput, calls=%fused_computation.16 | convolution fusion | flops 805568512 | bytes 1574912 | tf_op jit(solution)/shard_map/dot_general | solution.py:25
  10.2 0.6 convolution_bitcast_fusion.3
  10.8 0.0 copy-start.3
  10.8 17.5 %all_gather.12 = f32[512,256]{0,1:T(8,128)S(1)} all-gather(f32[128,256]{0,1:T(8,128)S(1)} %convolution_bitcast_fusion.3), channel_id=1, replica_groups=mesh['grp'=8,'leaf'=4] {'leaf'}, dimensions={0}, use_global_device_ids=true | all-gather | bytes 655360 | tf_op jit(solution)/shard_map/all_gather | solution.py:57
  28.3 0.6 fusion.30
  28.9 0.4 copy-done.5
  29.2 0.6 convolution_subtract_fusion.3
  29.8 0.4 copy-done.4
  30.2 1.2 convolution_bitcast_fusion.2
  31.4 0.0 reduce-scatter.3.cloned.1.call-update
  31.5 0.0 reduce-scatter.5.cloned.1.call-start
  31.5 21.3 %reduce-scatter.3.cloned.1.call-done = f32[128,64]{0,1:T(8,128)} async-done(((f32[128,256]{0,1:T(8,128)}), f32[128,64]{0,1:T(8,128)}) %reduce-scatter.3.cloned.1.call-update) | async-done | bytes 32784 | tf_op jit(solution)/shard_map/reduce_scatter | solution.py:61
  52.9 0.0 collective-permute-start
  52.9 4.4 %collective-permute-done = f32[128,64]{0,1:T(8,128)S(1)} collective-permute-done((f32[128,64]{0,1:T(8,128)}, f32[128,64]{0,1:T(8,128)S(1)}, u32[]{:S(2)}, u32[]{:S(2)}) %collective-permute-start) | collective-permute-done | bytes 32800 | tf_op jit(solution)/shard_map/ppermute | solution.py:17
  57.3 0.0 collective-permute-start.1
  57.3 2.6 %collective-permute-start.4 = (f32[128,64]{0,1:T(8,128)}, f32[128,64]{0,1:T(8,128)S(1)}, u32[]{:S(2)}, u32[]{:S(2)}) collective-permute-start(f32[128,64]{0,1:T(8,128)} %reduce-scatter.3.cloned.1.call-done), channel_id=1, source_target_pairs={{0,28},{4,0},{8,4},{12,8},{16,12},{20,16},{24,20},{28,24},{1,29},{... | collective-permute-start | bytes 98312 | tf_op jit(solution)/shard_map/ppermute | solution.py:19
  59.9 1.6 collective-permute-done.1
  61.5 0.0 collective-permute-start.2
  61.5 0.3 collective-permute-done.4
  61.9 2.5 %collective-permute-start.5 = (f32[128,64]{0,1:T(8,128)S(1)}, f32[128,64]{0,1:T(8,128)S(1)}, u32[]{:S(2)}, u32[]{:S(2)}) collective-permute-start(f32[128,64]{0,1:T(8,128)S(1)} %collective-permute-done.4), channel_id=1, source_target_pairs={{0,28},{4,0},{8,4},{12,8},{16,12},{20,16},{24,20},{28,24},{1,29},{... | collective-permute-start | bytes 98312 | tf_op jit(solution)/shard_map/ppermute | solution.py:19
  64.4 1.4 collective-permute-done.2
  65.8 0.0 collective-permute-start.3
  65.8 0.2 collective-permute-done.5
  66.0 2.6 %collective-permute-start.6 = (f32[128,64]{0,1:T(8,128)S(1)}, f32[128,64]{0,1:T(8,128)S(1)}, u32[]{:S(2)}, u32[]{:S(2)}) collective-permute-start(f32[128,64]{0,1:T(8,128)S(1)} %collective-permute-done.5), channel_id=1, source_target_pairs={{0,28},{4,0},{8,4},{12,8},{16,12},{20,16},{24,20},{28,24},{1,29},{... | collective-permute-start | bytes 98312 | tf_op jit(solution)/shard_map/ppermute | solution.py:19
  68.6 1.4 collective-permute-done.3
  70.1 0.8 constant_dynamic-update-slice_fusion.3
  70.8 0.0 collective-permute-done.6
  70.9 0.0 copy-start.7
  70.9 0.7 convolution_bitcast_fusion.5
  71.5 0.0 copy-start.10
  71.6 13.4 %all_gather.13 = f32[128,256]{0,1:T(8,128)S(1)} all-gather(f32[128,64]{0,1:T(8,128)S(1)} %convolution_bitcast_fusion.5), channel_id=1, replica_groups=mesh['grp'=8,'leaf'=4] {'leaf'}, dimensions={1}, use_global_device_ids=true | all-gather | bytes 163840 | tf_op jit(solution)/shard_map/all_gather | solution.py:63
  84.9 0.6 fusion.4
  85.6 1.2 fusion.8
  86.7 0.6 convolution_bitcast_fusion.1
  87.3 15.8 %all_gather.14 = f32[512,256]{0,1:T(8,128)S(1)} all-gather(f32[128,256]{0,1:T(8,128)S(1)} %convolution_bitcast_fusion.1), channel_id=1, replica_groups=mesh['grp'=8,'leaf'=4] {'leaf'}, dimensions={0}, use_global_device_ids=true | all-gather | bytes 655360 | tf_op jit(solution)/shard_map/all_gather | solution.py:57
  103.1 0.6 fusion.31
  103.7 0.4 copy-done.6
  104.1 0.6 convolution_subtract_fusion.1
  104.7 1.2 convolution_bitcast_fusion
  105.9 0.0 reduce-scatter.5.cloned.1.call-update
  105.9 16.9 %reduce-scatter.5.cloned.1.call-done = f32[128,64]{0,1:T(8,128)} async-done(((f32[128,256]{0,1:T(8,128)}), f32[128,64]{0,1:T(8,128)}) %reduce-scatter.5.cloned.1.call-update) | async-done | bytes 32784 | tf_op jit(solution)/shard_map/reduce_scatter | solution.py:61
  122.9 0.0 collective-permute-start.7
  122.9 4.4 %collective-permute-done.7 = f32[128,64]{0,1:T(8,128)S(1)} collective-permute-done((f32[128,64]{0,1:T(8,128)}, f32[128,64]{0,1:T(8,128)S(1)}, u32[]{:S(2)}, u32[]{:S(2)}) %collective-permute-start.7) | collective-permute-done | bytes 32800 | tf_op jit(solution)/shard_map/ppermute | solution.py:17
  127.3 0.0 collective-permute-start.8
  127.3 2.6 %collective-permute-start.11 = (f32[128,64]{0,1:T(8,128)}, f32[128,64]{0,1:T(8,128)S(1)}, u32[]{:S(2)}, u32[]{:S(2)}) collective-permute-start(f32[128,64]{0,1:T(8,128)} %reduce-scatter.5.cloned.1.call-done), channel_id=1, source_target_pairs={{0,28},{4,0},{8,4},{12,8},{16,12},{20,16},{24,20},{28,24},{1,29},{... | collective-permute-start | bytes 98312 | tf_op jit(solution)/shard_map/ppermute | solution.py:19
  130.0 1.6 collective-permute-done.8
  131.6 0.3 collective-permute-done.11
  131.9 2.5 %collective-permute-start.12 = (f32[128,64]{0,1:T(8,128)S(1)}, f32[128,64]{0,1:T(8,128)S(1)}, u32[]{:S(2)}, u32[]{:S(2)}) collective-permute-start(f32[128,64]{0,1:T(8,128)S(1)} %collective-permute-done.11), channel_id=1, source_target_pairs={{0,28},{4,0},{8,4},{12,8},{16,12},{20,16},{24,20},{28,24},{1,29},{... | collective-permute-start | bytes 98312 | tf_op jit(solution)/shard_map/ppermute | solution.py:19
  134.4 1.4 collective-permute-done.9
  135.8 0.0 collective-permute-start.10
  135.8 0.2 collective-permute-done.12
  136.0 2.6 %collective-permute-start.13 = (f32[128,64]{0,1:T(8,128)S(1)}, f32[128,64]{0,1:T(8,128)S(1)}, u32[]{:S(2)}, u32[]{:S(2)}) collective-permute-start(f32[128,64]{0,1:T(8,128)S(1)} %collective-permute-done.12), channel_id=1, source_target_pairs={{0,28},{4,0},{8,4},{12,8},{16,12},{20,16},{24,20},{28,24},{1,29},{... | collective-permute-start | bytes 98312 | tf_op jit(solution)/shard_map/ppermute | solution.py:19
  138.7 1.4 collective-permute-done.10
  140.1 0.7 copy-done.9
  140.8 0.0 collective-permute-done.13
  140.9 0.0 copy-start.8
  140.9 0.7 convolution_bitcast_fusion.4
  141.5 13.3 %all_gather.15 = f32[128,256]{0,1:T(8,128)S(1)} all-gather(f32[128,64]{0,1:T(8,128)S(1)} %convolution_bitcast_fusion.4), channel_id=1, replica_groups=mesh['grp'=8,'leaf'=4] {'leaf'}, dimensions={1}, use_global_device_ids=true | all-gather | bytes 163840 | tf_op jit(solution)/shard_map/all_gather | solution.py:63
  154.9 0.7 fusion.20
  155.6 1.0 copy.10
  156.6 1.0 copy.11
  (28 shorter events, 0.1 us)
Async XLA Ops:
  7.2 1.2 copy-start
  7.2 3.0 %copy-start.2 = (f32[512,128]{1,0:T(8,128)S(1)}, f32[512,128]{1,0:T(8,128)}, u32[]{:S(2)}) copy-start(f32[512,128]{1,0:T(8,128)} %param.12) | copy-start | bytes 786436
  7.2 45.7 %reduce-scatter.3.cloned.1.call-start = ((), (), s32[]{:S(2)}) async-start(), calls=%async_computation.2 | async-start | bytes 163840 | tf_op jit(solution)/shard_map/reduce_scatter | solution.py:61
  10.8 17.5 %copy-start.3 = (f32[128,512]{1,0:T(8,128)S(1)}, f32[128,512]{1,0:T(8,128)}, u32[]{:S(2)}) copy-start(f32[128,512]{1,0:T(8,128)} %param.14) | copy-start | bytes 786436
  28.3 1.0 copy-start.5
  29.2 0.9 copy-start.4
  31.4 39.4 %copy-start.1 = (f32[128,1024]{1,0:T(8,128)S(1)}, f32[128,1024]{1,0:T(8,128)}, u32[]{:S(2)}) copy-start(f32[128,1024]{1,0:T(8,128)} %param.17) | copy-start | bytes 1572868
  31.5 91.4 %reduce-scatter.5.cloned.1.call-start = ((), (), s32[]{:S(2)}) async-start(), calls=%async_computation.3 | async-start | bytes 163840 | tf_op jit(solution)/shard_map/reduce_scatter | solution.py:61
  52.9 4.4 %collective-permute-start = (f32[128,64]{0,1:T(8,128)}, f32[128,64]{0,1:T(8,128)S(1)}, u32[]{:S(2)}, u32[]{:S(2)}) collective-permute-start(f32[128,64]{0,1:T(8,128)} %reduce-scatter.3.cloned.1.call-done), channel_id=1, source_target_pairs={{0,4},{4,8},{8,12},{12,16},{16,20},{20,24},{24,28},{28,0},{1,5},{5... | collective-permute-start | bytes 98312 | tf_op jit(solution)/shard_map/ppermute | solution.py:17
  57.3 4.2 %collective-permute-start.1 = (f32[128,64]{0,1:T(8,128)S(1)}, f32[128,64]{0,1:T(8,128)S(1)}, u32[]{:S(2)}, u32[]{:S(2)}) collective-permute-start(f32[128,64]{0,1:T(8,128)S(1)} %collective-permute-done), channel_id=1, source_target_pairs={{0,4},{4,8},{8,12},{12,16},{16,20},{20,24},{24,28},{28,0},{1,5},{5... | collective-permute-start | bytes 98312 | tf_op jit(solution)/shard_map/ppermute | solution.py:17
  57.3 4.6 %collective-permute-start.4 = (f32[128,64]{0,1:T(8,128)}, f32[128,64]{0,1:T(8,128)S(1)}, u32[]{:S(2)}, u32[]{:S(2)}) collective-permute-start(f32[128,64]{0,1:T(8,128)} %reduce-scatter.3.cloned.1.call-done), channel_id=1, source_target_pairs={{0,28},{4,0},{8,4},{12,8},{16,12},{20,16},{24,20},{28,24},{1,29},{... | collective-permute-start | bytes 98312 | tf_op jit(solution)/shard_map/ppermute | solution.py:19
  61.5 4.2 %collective-permute-start.2 = (f32[128,64]{0,1:T(8,128)S(1)}, f32[128,64]{0,1:T(8,128)S(1)}, u32[]{:S(2)}, u32[]{:S(2)}) collective-permute-start(f32[128,64]{0,1:T(8,128)S(1)} %collective-permute-done.1), channel_id=1, source_target_pairs={{0,4},{4,8},{8,12},{12,16},{16,20},{20,24},{24,28},{28,0},{1,5},{5... | collective-permute-start | bytes 98312 | tf_op jit(solution)/shard_map/ppermute | solution.py:17
  61.9 4.1 %collective-permute-start.5 = (f32[128,64]{0,1:T(8,128)S(1)}, f32[128,64]{0,1:T(8,128)S(1)}, u32[]{:S(2)}, u32[]{:S(2)}) collective-permute-start(f32[128,64]{0,1:T(8,128)S(1)} %collective-permute-done.4), channel_id=1, source_target_pairs={{0,28},{4,0},{8,4},{12,8},{16,12},{20,16},{24,20},{28,24},{1,29},{... | collective-permute-start | bytes 98312 | tf_op jit(solution)/shard_map/ppermute | solution.py:19
  65.8 4.2 %collective-permute-start.3 = (f32[128,64]{0,1:T(8,128)S(1)}, f32[128,64]{0,1:T(8,128)S(1)}, u32[]{:S(2)}, u32[]{:S(2)}) collective-permute-start(f32[128,64]{0,1:T(8,128)S(1)} %collective-permute-done.2), channel_id=1, source_target_pairs={{0,4},{4,8},{8,12},{12,16},{16,20},{20,24},{24,28},{28,0},{1,5},{5... | collective-permute-start | bytes 98312 | tf_op jit(solution)/shard_map/ppermute | solution.py:17
  66.0 4.8 %collective-permute-start.6 = (f32[128,64]{0,1:T(8,128)S(1)}, f32[128,64]{0,1:T(8,128)S(1)}, u32[]{:S(2)}, u32[]{:S(2)}) collective-permute-start(f32[128,64]{0,1:T(8,128)S(1)} %collective-permute-done.5), channel_id=1, source_target_pairs={{0,28},{4,0},{8,4},{12,8},{16,12},{20,16},{24,20},{28,24},{1,29},{... | collective-permute-start | bytes 98312 | tf_op jit(solution)/shard_map/ppermute | solution.py:19
  70.9 14.1 %copy-start.7 = (f32[512,128]{1,0:T(8,128)S(1)}, f32[512,128]{1,0:T(8,128)}, u32[]{:S(2)}) copy-start(f32[512,128]{1,0:T(8,128)} %param.16) | copy-start | bytes 786436
  71.5 13.4 %copy-start.10 = (s32[512]{0:T(512)S(1)}, s32[512]{0:T(512)}, u32[]{:S(2)}) copy-start(s32[512]{0:T(512)} %param.10) | copy-start | bytes 6148
  103.1 1.0 copy-start.6
  122.9 4.4 %collective-permute-start.7 = (f32[128,64]{0,1:T(8,128)}, f32[128,64]{0,1:T(8,128)S(1)}, u32[]{:S(2)}, u32[]{:S(2)}) collective-permute-start(f32[128,64]{0,1:T(8,128)} %reduce-scatter.5.cloned.1.call-done), channel_id=1, source_target_pairs={{0,4},{4,8},{8,12},{12,16},{16,20},{20,24},{24,28},{28,0},{1,5},{5... | collective-permute-start | bytes 98312 | tf_op jit(solution)/shard_map/ppermute | solution.py:17
  127.3 4.2 %collective-permute-start.8 = (f32[128,64]{0,1:T(8,128)S(1)}, f32[128,64]{0,1:T(8,128)S(1)}, u32[]{:S(2)}, u32[]{:S(2)}) collective-permute-start(f32[128,64]{0,1:T(8,128)S(1)} %collective-permute-done.7), channel_id=1, source_target_pairs={{0,4},{4,8},{8,12},{12,16},{16,20},{20,24},{24,28},{28,0},{1,5},{5... | collective-permute-start | bytes 98312 | tf_op jit(solution)/shard_map/ppermute | solution.py:17
  127.3 4.6 %collective-permute-start.11 = (f32[128,64]{0,1:T(8,128)}, f32[128,64]{0,1:T(8,128)S(1)}, u32[]{:S(2)}, u32[]{:S(2)}) collective-permute-start(f32[128,64]{0,1:T(8,128)} %reduce-scatter.5.cloned.1.call-done), channel_id=1, source_target_pairs={{0,28},{4,0},{8,4},{12,8},{16,12},{20,16},{24,20},{28,24},{1,29},{... | collective-permute-start | bytes 98312 | tf_op jit(solution)/shard_map/ppermute | solution.py:19
  131.6 4.2 %collective-permute-start.9 = (f32[128,64]{0,1:T(8,128)S(1)}, f32[128,64]{0,1:T(8,128)S(1)}, u32[]{:S(2)}, u32[]{:S(2)}) collective-permute-start(f32[128,64]{0,1:T(8,128)S(1)} %collective-permute-done.8), channel_id=1, source_target_pairs={{0,4},{4,8},{8,12},{12,16},{16,20},{20,24},{24,28},{28,0},{1,5},{5... | collective-permute-start | bytes 98312 | tf_op jit(solution)/shard_map/ppermute | solution.py:17
  131.9 4.1 %collective-permute-start.12 = (f32[128,64]{0,1:T(8,128)S(1)}, f32[128,64]{0,1:T(8,128)S(1)}, u32[]{:S(2)}, u32[]{:S(2)}) collective-permute-start(f32[128,64]{0,1:T(8,128)S(1)} %collective-permute-done.11), channel_id=1, source_target_pairs={{0,28},{4,0},{8,4},{12,8},{16,12},{20,16},{24,20},{28,24},{1,29},{... | collective-permute-start | bytes 98312 | tf_op jit(solution)/shard_map/ppermute | solution.py:19
  135.8 4.2 %collective-permute-start.10 = (f32[128,64]{0,1:T(8,128)S(1)}, f32[128,64]{0,1:T(8,128)S(1)}, u32[]{:S(2)}, u32[]{:S(2)}) collective-permute-start(f32[128,64]{0,1:T(8,128)S(1)} %collective-permute-done.9), channel_id=1, source_target_pairs={{0,4},{4,8},{8,12},{12,16},{16,20},{20,24},{24,28},{28,0},{1,5},{5... | collective-permute-start | bytes 98312 | tf_op jit(solution)/shard_map/ppermute | solution.py:17
  136.0 4.8 %collective-permute-start.13 = (f32[128,64]{0,1:T(8,128)S(1)}, f32[128,64]{0,1:T(8,128)S(1)}, u32[]{:S(2)}, u32[]{:S(2)}) collective-permute-start(f32[128,64]{0,1:T(8,128)S(1)} %collective-permute-done.12), channel_id=1, source_target_pairs={{0,28},{4,0},{8,4},{12,8},{16,12},{20,16},{24,20},{28,24},{1,29},{... | collective-permute-start | bytes 98312 | tf_op jit(solution)/shard_map/ppermute | solution.py:19
  140.1 0.8 copy-start.9
  140.9 14.0 %copy-start.8 = (f32[512,128]{1,0:T(8,128)S(1)}, f32[512,128]{1,0:T(8,128)}, u32[]{:S(2)}) copy-start(f32[512,128]{1,0:T(8,128)} %param.16) | copy-start | bytes 786436
Sparse Core Ops, SparseCore 0:
  31.6 21.2 reduce-scatter.2
  106.0 16.7 reduce-scatter.4
